TPU v7x, 256 devices: a whole 4x4x8 slice. The times are simulated.
256 devices in a mesh: depth: 8 (over x, z_lo), sky: 32 (over y, z_hi, core).
Axes of the slice: x: 4, y: 4, z: 8 (z_hi: 4, z_lo: 2; z = z_hi * 2 + z_lo), core: 2. Of those that a mesh axis runs over, the one named last changes fastest.
Arguments:
- potential: float32 [96, 1024, 2048], P('depth', 'sky'), may hold values from -6 to 6
- widths: int32 [96], P('depth'), may hold values from 1 to 8, as said below
- plane_slot: int32 [96], P('depth'), may hold values from 0 to 15
- ratio_near: float32 [16], replicated, may hold values from 1 to 1.6
- ratio_lens: float32 [16], replicated, may hold values from 0.5 to 1.5
Outputs:
- convergence: float32 [96, 1024, 2048], P('depth', 'sky')
Inputs may be any that keep to these rules, and one draw needn't show every extreme that they name: `widths`: some plane has half-width 8.
All inputs are finite; a program needn't handle non-finite values.
Results may differ from a plain program's by a relative error of at most 0.0003.
Values sent between devices are 32-bit elements; how exact they have to be, the bound alone decides.
A program may use at most 64 MiB of HBM per device.

v0:
```python
import jax
import jax.numpy as jnp
from jax import lax
from jax.sharding import PartitionSpec as P

WMAX = 8
TILE = 512


def padded_2(x, sides, width):
    for axis, dim in sides:
        devices, length = (lax.axis_size(axis), x.shape[dim])
        up = [(i, (i + 1) % devices) for i in range(devices - 1)]
        down = [(j, i) for i, j in up]
        last = lax.slice_in_dim(x, length - width, length, axis=dim)
        first = lax.slice_in_dim(x, 0, width, axis=dim)
        before = lax.ppermute(last, axis, up)
        after = lax.ppermute(first, axis, down)
        x = jnp.concatenate([before, x, after], axis=dim)
    return x


def passed_along(value, axis, steps):
    count = lax.axis_size(axis)
    first, last = (max(0, -steps), min(count, count - steps))
    return lax.ppermute(value, axis, [(source, source + steps) for source in range(first, last)])


def box_filter(values, half_width, axis_index, length):
    summed = None
    for displace in range(-WMAX, WMAX + 1):
        window = lax.slice_in_dim(
            values, WMAX + displace, WMAX + displace + length, axis=axis_index
        )
        active = jnp.where(abs(displace) <= half_width, 1.0, 0.0).astype(jnp.float32)
        term = active * window
        summed = term if summed is None else summed + term
    return summed / (2.0 * half_width.astype(jnp.float32) + 1.0)


def hessian(padded, half_width, row_count, col_count):
    along = box_filter(padded, half_width, 0, row_count + 2)
    smooth = box_filter(along, half_width, 1, col_count + 2)
    centre = smooth[1:-1, 1:-1]
    along_cols = smooth[1:-1, 2:] - 2.0 * centre + smooth[1:-1, :-2]
    along_rows = smooth[2:, 1:-1] - 2.0 * centre + smooth[:-2, 1:-1]
    mixed_term = 0.25 * (smooth[2:, 2:] - smooth[2:, :-2] - smooth[:-2, 2:] + smooth[:-2, :-2])
    return (along_cols, along_rows, mixed_term)


def advance(carried, along_cols, along_rows, mixed_term, near_factor, lens_factor):
    entry_xx = near_factor - lens_factor * along_cols
    entry_yy = near_factor - lens_factor * along_rows
    entry_xy = -lens_factor * mixed_term
    retained = 1.0 - near_factor
    upper = carried[0:2]
    lower = carried[2:4]
    row_first = entry_xx * upper[0] + entry_xy * upper[1] + retained * lower[0]
    row_second = entry_xy * upper[0] + entry_yy * upper[1] + retained * lower[1]
    advanced = jnp.stack([row_first, row_second, upper[0], upper[1]])
    convergence = 1.0 - 0.5 * (row_first[0] + row_second[1])
    return (advanced, convergence)


def identity_state(row_count, col_count):
    pattern = jnp.array([[1.0, 0.0], [0.0, 1.0], [1.0, 0.0], [0.0, 1.0]], dtype=jnp.float32)
    return jnp.broadcast_to(pattern[:, :, None, None], (4, 2, row_count, col_count))


def propagate(carried, curvatures, near_factor, lens_factor):

    def plane(loop_state, inputs):
        along_cols, along_rows, mixed_term, near_one, lens_one = inputs
        return advance(loop_state, along_cols, along_rows, mixed_term, near_one, lens_one)

    return lax.scan(
        plane, carried, (curvatures[0], curvatures[1], curvatures[2], near_factor, lens_factor)
    )


def factors_of(slots, ratio_near, ratio_lens):
    table_ids = jnp.arange(ratio_near.shape[0], dtype=jnp.int32)
    chosen = (slots[:, None] == table_ids[None, :]).astype(jnp.float32)
    near_factor = jnp.sum(chosen * ratio_near[None, :], axis=1)
    lens_factor = jnp.sum(chosen * ratio_lens[None, :], axis=1)
    return (near_factor, lens_factor)


def per_device(potential, widths, plane_slot, ratio_near, ratio_lens):
    planes = potential.shape[0]
    row_count = potential.shape[1]
    col_count = potential.shape[2]
    rim_rows = WMAX + 1
    extended = padded_2(potential, (("sky", 1),), rim_rows)
    depth_index = lax.axis_index("depth")
    depth_count = lax.axis_size("depth")
    is_first = depth_index == 0

    def curvature(inputs):
        plane_map, half_width = inputs
        padded = jnp.pad(plane_map, ((0, 0), (rim_rows, rim_rows)))
        return hessian(padded, half_width, row_count, col_count)

    curvatures = lax.map(curvature, (extended, widths))
    near_factor, lens_factor = factors_of(plane_slot, ratio_near, ratio_lens)
    tile_cols = TILE
    tile_count = col_count // tile_cols
    initial = identity_state(row_count, tile_cols)

    def tick(tick_index, loop_state):
        outgoing, gathered = loop_state
        received = passed_along(outgoing, "depth", 1)
        incoming = jnp.where(is_first, initial, received)
        column = tick_index - depth_index
        inside = (column >= 0) & (column < tile_count)
        offset = jnp.clip(column, 0, tile_count - 1) * tile_cols
        pieces = tuple(
            (lax.dynamic_slice_in_dim(member, offset, tile_cols, 2) for member in curvatures)
        )
        result, tile_values = propagate(incoming, pieces, near_factor, lens_factor)
        previous = lax.dynamic_slice_in_dim(gathered, offset, tile_cols, 2)
        gathered = lax.dynamic_update_slice_in_dim(
            gathered, jnp.where(inside, tile_values, previous), offset, 2
        )
        return (result, gathered)

    empty = jnp.zeros((planes, row_count, col_count), jnp.float32)
    final_state, convergence = lax.fori_loop(
        0, tile_count + depth_count - 1, tick, (initial, empty)
    )
    return convergence


def solution(mesh):
    return jax.shard_map(
        per_device,
        mesh=mesh,
        in_specs=(P("depth", "sky", None), P("depth"), P("depth"), P(), P()),
        out_specs=P("depth", "sky", None),
        check_vma=False,
    )
```

profile of v0, /device:TPU:119, one launch (start us, length us, event | category | flops | bytes accessed | tf_op | source)
XLA Modules:
  0.0 1125.9 jit_solution(835769867564638182)
XLA Ops:
  3.8 5.8 collective-permute-start.1
  13.5 20.2 %collective-permute-done.1 = f32[12,9,2048]{2,0,1:T(8,128)} collective-permute-done((f32[12,9,2048]{2,0,1:T(8,128)}, f32[12,9,2048]{2,0,1:T(8,128)}, u32[]{:S(2)}, u32[]{:S(2)}) %collective-permute-start.1) | collective-permute-done | bytes 884768 | tf_op jit(solution)/shard_map/ppermute | solution.py:17
  35.6 7.9 collective-permute-done.2
  45.3 3.1 pad_maximum_fusion.1
  52.9 150.5 %while.60 = (s32[]{:T(128)}, f32[12,32,2048]{2,1,0:T(8,128)S(1)}, f32[12,32,2048]{2,1,0:T(8,128)}, f32[12,32,2048]{2,1,0:T(8,128)}, s32[12]{0:T(128)S(1)}, /*ind...) while((s32[]{:T(128)}, f32[12,32,2048]{2,1,0:T(8,128)S(1)}, ...), condition=%wide.region_1.2_spmd, body=%wide.region_0.1_spmd.sunk | while | flops 5347943 | bytes 9674915 | solution.py:104
  207.1 918.8 %while.62 = (s32[]{:T(128)}, f32[4,2,32,512]{3,2,1,0:T(8,128)S(1)}, f32[12,32,2048]{2,1,0:T(8,128)}, pred[]{:T(512)}, s32[]{:T(128)}, /*index=5*/f32[12,32,2048]...) while((s32[]{:T(128)}, f32[4,2,32,512]{3,2,1,0:T(8,128)S(1)}, ...), condition=%wide.region_7.8_spmd.clone, body=%wide.region_4.7_spmd.sunk.clone.sunk | while | flops 1179664 | bytes 14353523 | solution.py:128
  211.3 6.0 collective-permute-done
  217.4 67.4 %while.63 = (s32[]{:T(128)}, f32[4,2,32,512]{3,2,1,0:T(8,128)S(1)}, f32[12,32,512]{2,1,0:T(8,128)}, f32[12]{0:T(128)S(1)}, f32[12]{0:T(128)S(1)}, /*index=5*/f32...) while((s32[]{:T(128)}, f32[4,2,32,512]{3,2,1,0:T(8,128)S(1)}, ...), condition=%wide.region_6.6_spmd, body=%wide.region_5.5_spmd.sunk | while | flops 851972 | bytes 4129457 | solution.py:76
  291.0 8.6 collective-permute-done
  299.7 67.4 %while.63 = (s32[]{:T(128)}, f32[4,2,32,512]{3,2,1,0:T(8,128)S(1)}, f32[12,32,512]{2,1,0:T(8,128)}, f32[12]{0:T(128)S(1)}, f32[12]{0:T(128)S(1)}, /*index=5*/f32...) while((s32[]{:T(128)}, f32[4,2,32,512]{3,2,1,0:T(8,128)S(1)}, ...), condition=%wide.region_6.6_spmd, body=%wide.region_5.5_spmd.sunk | while | flops 851972 | bytes 4129457 | solution.py:76
  373.4 9.7 collective-permute-done
  383.2 67.4 %while.63 = (s32[]{:T(128)}, f32[4,2,32,512]{3,2,1,0:T(8,128)S(1)}, f32[12,32,512]{2,1,0:T(8,128)}, f32[12]{0:T(128)S(1)}, f32[12]{0:T(128)S(1)}, /*index=5*/f32...) while((s32[]{:T(128)}, f32[4,2,32,512]{3,2,1,0:T(8,128)S(1)}, ...), condition=%wide.region_6.6_spmd, body=%wide.region_5.5_spmd.sunk | while | flops 851972 | bytes 4129457 | solution.py:76
  456.9 10.9 collective-permute-done
  467.9 67.4 %while.63 = (s32[]{:T(128)}, f32[4,2,32,512]{3,2,1,0:T(8,128)S(1)}, f32[12,32,512]{2,1,0:T(8,128)}, f32[12]{0:T(128)S(1)}, f32[12]{0:T(128)S(1)}, /*index=5*/f32...) while((s32[]{:T(128)}, f32[4,2,32,512]{3,2,1,0:T(8,128)S(1)}, ...), condition=%wide.region_6.6_spmd, body=%wide.region_5.5_spmd.sunk | while | flops 851972 | bytes 4129457 | solution.py:76
  541.6 12.0 %collective-permute-done = f32[4,2,32,512]{3,2,1,0:T(8,128)S(1)} collective-permute-done((f32[4,2,32,512]{3,2,1,0:T(8,128)S(1)}, f32[4,2,32,512]{3,2,1,0:T(8,128)S(1)}, u32[]{:S(2)}, u32[]{:S(2)}) %collective-permute-start) | collective-permute-done | bytes 524320 | tf_op jit(solution)/shard_map/while/body/eval_jaxpr/ppermute | solution.py:26
  553.7 67.4 %while.63 = (s32[]{:T(128)}, f32[4,2,32,512]{3,2,1,0:T(8,128)S(1)}, f32[12,32,512]{2,1,0:T(8,128)}, f32[12]{0:T(128)S(1)}, f32[12]{0:T(128)S(1)}, /*index=5*/f32...) while((s32[]{:T(128)}, f32[4,2,32,512]{3,2,1,0:T(8,128)S(1)}, ...), condition=%wide.region_6.6_spmd, body=%wide.region_5.5_spmd.sunk | while | flops 851972 | bytes 4129457 | solution.py:76
  627.4 12.4 %collective-permute-done = f32[4,2,32,512]{3,2,1,0:T(8,128)S(1)} collective-permute-done((f32[4,2,32,512]{3,2,1,0:T(8,128)S(1)}, f32[4,2,32,512]{3,2,1,0:T(8,128)S(1)}, u32[]{:S(2)}, u32[]{:S(2)}) %collective-permute-start) | collective-permute-done | bytes 524320 | tf_op jit(solution)/shard_map/while/body/eval_jaxpr/ppermute | solution.py:26
  639.9 67.4 %while.63 = (s32[]{:T(128)}, f32[4,2,32,512]{3,2,1,0:T(8,128)S(1)}, f32[12,32,512]{2,1,0:T(8,128)}, f32[12]{0:T(128)S(1)}, f32[12]{0:T(128)S(1)}, /*index=5*/f32...) while((s32[]{:T(128)}, f32[4,2,32,512]{3,2,1,0:T(8,128)S(1)}, ...), condition=%wide.region_6.6_spmd, body=%wide.region_5.5_spmd.sunk | while | flops 851972 | bytes 4129457 | solution.py:76
  713.6 11.0 collective-permute-done
  724.7 67.4 %while.63 = (s32[]{:T(128)}, f32[4,2,32,512]{3,2,1,0:T(8,128)S(1)}, f32[12,32,512]{2,1,0:T(8,128)}, f32[12]{0:T(128)S(1)}, f32[12]{0:T(128)S(1)}, /*index=5*/f32...) while((s32[]{:T(128)}, f32[4,2,32,512]{3,2,1,0:T(8,128)S(1)}, ...), condition=%wide.region_6.6_spmd, body=%wide.region_5.5_spmd.sunk | while | flops 851972 | bytes 4129457 | solution.py:76
  798.3 10.3 collective-permute-done
  808.8 67.4 %while.63 = (s32[]{:T(128)}, f32[4,2,32,512]{3,2,1,0:T(8,128)S(1)}, f32[12,32,512]{2,1,0:T(8,128)}, f32[12]{0:T(128)S(1)}, f32[12]{0:T(128)S(1)}, /*index=5*/f32...) while((s32[]{:T(128)}, f32[4,2,32,512]{3,2,1,0:T(8,128)S(1)}, ...), condition=%wide.region_6.6_spmd, body=%wide.region_5.5_spmd.sunk | while | flops 851972 | bytes 4129457 | solution.py:76
  876.2 2.4 select_dynamic-update-slice_fusion.2
  882.7 9.3 collective-permute-done
  892.1 67.4 %while.63 = (s32[]{:T(128)}, f32[4,2,32,512]{3,2,1,0:T(8,128)S(1)}, f32[12,32,512]{2,1,0:T(8,128)}, f32[12]{0:T(128)S(1)}, f32[12]{0:T(128)S(1)}, /*index=5*/f32...) while((s32[]{:T(128)}, f32[4,2,32,512]{3,2,1,0:T(8,128)S(1)}, ...), condition=%wide.region_6.6_spmd, body=%wide.region_5.5_spmd.sunk | while | flops 851972 | bytes 4129457 | solution.py:76
  959.5 2.4 select_dynamic-update-slice_fusion.2
  966.0 8.4 collective-permute-done
  974.5 67.4 %while.63 = (s32[]{:T(128)}, f32[4,2,32,512]{3,2,1,0:T(8,128)S(1)}, f32[12,32,512]{2,1,0:T(8,128)}, f32[12]{0:T(128)S(1)}, f32[12]{0:T(128)S(1)}, /*index=5*/f32...) while((s32[]{:T(128)}, f32[4,2,32,512]{3,2,1,0:T(8,128)S(1)}, ...), condition=%wide.region_6.6_spmd, body=%wide.region_5.5_spmd.sunk | while | flops 851972 | bytes 4129457 | solution.py:76
  1041.9 2.4 select_dynamic-update-slice_fusion.2
  1048.4 7.5 collective-permute-done
  1056.1 67.4 %while.63 = (s32[]{:T(128)}, f32[4,2,32,512]{3,2,1,0:T(8,128)S(1)}, f32[12,32,512]{2,1,0:T(8,128)}, f32[12]{0:T(128)S(1)}, f32[12]{0:T(128)S(1)}, /*index=5*/f32...) while((s32[]{:T(128)}, f32[4,2,32,512]{3,2,1,0:T(8,128)S(1)}, ...), condition=%wide.region_6.6_spmd, body=%wide.region_5.5_spmd.sunk | while | flops 851972 | bytes 4129457 | solution.py:76
  1123.5 2.4 select_dynamic-update-slice_fusion.2
  (1204 shorter events, 731.4 us)
Async XLA Ops:
  2.2 11.1 copy-start.3
  2.2 11.1 copy-start.4
  2.2 11.1 copy-start.5
  3.8 30.0 %collective-permute-start.1 = (f32[12,9,2048]{2,0,1:T(8,128)}, f32[12,9,2048]{2,0,1:T(8,128)}, u32[]{:S(2)}, u32[]{:S(2)}) collective-permute-start(f32[12,9,2048]{2,0,1:T(8,128)} %copy.15), channel_id=1, source_target_pairs={{0,1},{1,2},{2,3},{3,4},{4,5},{5,6},{6,7},{7,8},{8,9},{9,10},{10,1... | collective-permute-start | bytes 2654216 | tf_op jit(solution)/shard_map/ppermute | solution.py:17
  11.1 34.2 %copy-start.1 = (f32[12,32,2048]{2,1,0:T(8,128)S(1)}, f32[12,32,2048]{2,1,0:T(8,128)}, u32[]{:S(2)}) copy-start(f32[12,32,2048]{2,1,0:T(8,128)} %param.12) | copy-start | bytes 9437188
  11.1 32.4 %collective-permute-start.2 = (f32[12,9,2048]{2,0,1:T(8,128)}, f32[12,9,2048]{2,0,1:T(8,128)}, u32[]{:S(2)}, u32[]{:S(2)}) collective-permute-start(f32[12,9,2048]{2,0,1:T(8,128)} %copy.16), channel_id=1, source_target_pairs={{1,0},{2,1},{3,2},{4,3},{5,4},{6,5},{7,6},{8,7},{9,8},{10,9},{11,1... | collective-permute-start | bytes 2654216 | tf_op jit(solution)/shard_map/ppermute | solution.py:18
  48.7 4.2 copy-start.6
  203.4 1.6 copy-start
  203.4 3.7 copy-start.2
  207.2 10.1 collective-permute-start
  287.0 12.7 %collective-permute-start = (f32[4,2,32,512]{3,2,1,0:T(8,128)S(1)}, f32[4,2,32,512]{3,2,1,0:T(8,128)S(1)}, u32[]{:S(2)}, u32[]{:S(2)}) collective-permute-start(f32[4,2,32,512]{3,2,1,0:T(8,128)S(1)} %get-tuple-element.722), channel_id=1, source_target_pairs={{0,32},{32,64},{64,96},{96,128},{128,160},{160,192},{192,224},{1,3... | collective-permute-start | bytes 1572872 | tf_op jit(solution)/shard_map/while/body/eval_jaxpr/ppermute | solution.py:26
  369.3 13.8 %collective-permute-start = (f32[4,2,32,512]{3,2,1,0:T(8,128)S(1)}, f32[4,2,32,512]{3,2,1,0:T(8,128)S(1)}, u32[]{:S(2)}, u32[]{:S(2)}) collective-permute-start(f32[4,2,32,512]{3,2,1,0:T(8,128)S(1)} %get-tuple-element.722), channel_id=1, source_target_pairs={{0,32},{32,64},{64,96},{96,128},{128,160},{160,192},{192,224},{1,3... | collective-permute-start | bytes 1572872 | tf_op jit(solution)/shard_map/while/body/eval_jaxpr/ppermute | solution.py:26
  452.8 15.0 %collective-permute-start = (f32[4,2,32,512]{3,2,1,0:T(8,128)S(1)}, f32[4,2,32,512]{3,2,1,0:T(8,128)S(1)}, u32[]{:S(2)}, u32[]{:S(2)}) collective-permute-start(f32[4,2,32,512]{3,2,1,0:T(8,128)S(1)} %get-tuple-element.722), channel_id=1, source_target_pairs={{0,32},{32,64},{64,96},{96,128},{128,160},{160,192},{192,224},{1,3... | collective-permute-start | bytes 1572872 | tf_op jit(solution)/shard_map/while/body/eval_jaxpr/ppermute | solution.py:26
  537.5 16.1 %collective-permute-start = (f32[4,2,32,512]{3,2,1,0:T(8,128)S(1)}, f32[4,2,32,512]{3,2,1,0:T(8,128)S(1)}, u32[]{:S(2)}, u32[]{:S(2)}) collective-permute-start(f32[4,2,32,512]{3,2,1,0:T(8,128)S(1)} %get-tuple-element.722), channel_id=1, source_target_pairs={{0,32},{32,64},{64,96},{96,128},{128,160},{160,192},{192,224},{1,3... | collective-permute-start | bytes 1572872 | tf_op jit(solution)/shard_map/while/body/eval_jaxpr/ppermute | solution.py:26
  623.3 16.5 %collective-permute-start = (f32[4,2,32,512]{3,2,1,0:T(8,128)S(1)}, f32[4,2,32,512]{3,2,1,0:T(8,128)S(1)}, u32[]{:S(2)}, u32[]{:S(2)}) collective-permute-start(f32[4,2,32,512]{3,2,1,0:T(8,128)S(1)} %get-tuple-element.722), channel_id=1, source_target_pairs={{0,32},{32,64},{64,96},{96,128},{128,160},{160,192},{192,224},{1,3... | collective-permute-start | bytes 1572872 | tf_op jit(solution)/shard_map/while/body/eval_jaxpr/ppermute | solution.py:26
  709.5 15.0 %collective-permute-start = (f32[4,2,32,512]{3,2,1,0:T(8,128)S(1)}, f32[4,2,32,512]{3,2,1,0:T(8,128)S(1)}, u32[]{:S(2)}, u32[]{:S(2)}) collective-permute-start(f32[4,2,32,512]{3,2,1,0:T(8,128)S(1)} %get-tuple-element.722), channel_id=1, source_target_pairs={{0,32},{32,64},{64,96},{96,128},{128,160},{160,192},{192,224},{1,3... | collective-permute-start | bytes 1572872 | tf_op jit(solution)/shard_map/while/body/eval_jaxpr/ppermute | solution.py:26
  794.3 14.4 %collective-permute-start = (f32[4,2,32,512]{3,2,1,0:T(8,128)S(1)}, f32[4,2,32,512]{3,2,1,0:T(8,128)S(1)}, u32[]{:S(2)}, u32[]{:S(2)}) collective-permute-start(f32[4,2,32,512]{3,2,1,0:T(8,128)S(1)} %get-tuple-element.722), channel_id=1, source_target_pairs={{0,32},{32,64},{64,96},{96,128},{128,160},{160,192},{192,224},{1,3... | collective-permute-start | bytes 1572872 | tf_op jit(solution)/shard_map/while/body/eval_jaxpr/ppermute | solution.py:26
  878.6 13.3 %collective-permute-start = (f32[4,2,32,512]{3,2,1,0:T(8,128)S(1)}, f32[4,2,32,512]{3,2,1,0:T(8,128)S(1)}, u32[]{:S(2)}, u32[]{:S(2)}) collective-permute-start(f32[4,2,32,512]{3,2,1,0:T(8,128)S(1)} %get-tuple-element.722), channel_id=1, source_target_pairs={{0,32},{32,64},{64,96},{96,128},{128,160},{160,192},{192,224},{1,3... | collective-permute-start | bytes 1572872 | tf_op jit(solution)/shard_map/while/body/eval_jaxpr/ppermute | solution.py:26
  961.9 12.5 %collective-permute-start = (f32[4,2,32,512]{3,2,1,0:T(8,128)S(1)}, f32[4,2,32,512]{3,2,1,0:T(8,128)S(1)}, u32[]{:S(2)}, u32[]{:S(2)}) collective-permute-start(f32[4,2,32,512]{3,2,1,0:T(8,128)S(1)} %get-tuple-element.722), channel_id=1, source_target_pairs={{0,32},{32,64},{64,96},{96,128},{128,160},{160,192},{192,224},{1,3... | collective-permute-start | bytes 1572872 | tf_op jit(solution)/shard_map/while/body/eval_jaxpr/ppermute | solution.py:26
  1044.3 11.6 %collective-permute-start = (f32[4,2,32,512]{3,2,1,0:T(8,128)S(1)}, f32[4,2,32,512]{3,2,1,0:T(8,128)S(1)}, u32[]{:S(2)}, u32[]{:S(2)}) collective-permute-start(f32[4,2,32,512]{3,2,1,0:T(8,128)S(1)} %get-tuple-element.722), channel_id=1, source_target_pairs={{0,32},{32,64},{64,96},{96,128},{128,160},{160,192},{192,224},{1,3... | collective-permute-start | bytes 1572872 | tf_op jit(solution)/shard_map/while/body/eval_jaxpr/ppermute | solution.py:26
where the time goes:
time: 1140 us; the launch traced here: 1130 us
  other arithmetic  502 us (44%)
  loops' own time  242 us (21%)
  local copies, waits for them, and re-layouts  226 us (20%)
  waiting for transfers between devices  134 us (12%)
  starting transfers between devices  22 us (2%)
    mul x264, other arithmetic, advance(): row_first = entry_xx * upper[0] + entry_xy * upper[1] + retained * lower[0]  169 us
    another operation x11, loops' own time, propagate(): lax.scan(plane, carried, (curvatures[0], curvatures[1], curvatures[2], ne...  163 us
    mul x132, other arithmetic, advance(): row_second = entry_xy * upper[0] + entry_yy * upper[1] + retained * lower[1]  157 us
    dynamic_slice x264, local copies, waits for them, and re-layouts, propagate(): lax.scan(plane, carried, (curvatures[0], curvatures[1], curvatures[2], ne...  157 us
    ppermute x11, waiting for transfers between devices, passed_along(): lax.ppermute(value, axis, [(source, source + steps) for source in range(f...  106 us
    dynamic_update_slice x132, other arithmetic, propagate(): lax.scan(plane, carried, (curvatures[0], curvatures[1], curvatures[2], ne...  88.8 us
    another operation x1, loops' own time, per_device(): curvatures = lax.map(curvature, (extended, widths))  78.1 us
    div x24, other arithmetic, box_filter(): return summed / (2.0 * half_width.astype(jnp.float32) + 1.0)  37.6 us
  transfers between devices with their start and end apart: 13, of which 13 were waited for; matrix products, arithmetic and copies ran while one was open for 3% of the time, Pallas kernels for 0%

commit v1 on v0

v1 whole, which is shorter than its diff:
```python
import jax
import jax.numpy as jnp
from jax import lax
from jax.experimental import pallas as pl
from jax.experimental.pallas import tpu as pltpu
from jax.sharding import PartitionSpec as P

WMAX = 8
LANES = 128
EIGHT = 8
TILE = 256
FAR = 1000
MESH = pl.DeviceIdType.MESH
F32 = jnp.float32
BF16 = jnp.bfloat16


def round_up(value, step):
    return -(-value // step) * step


def split(values):
    high = values.astype(BF16)
    return high, (values - high.astype(F32)).astype(BF16)


def stencils(distance, half_width):
    inside = lambda shift: jnp.where(jnp.abs(distance + shift) <= half_width, 1.0, 0.0)
    after, here, before = inside(-1), inside(0), inside(1)
    return here.astype(BF16), (after - 2.0 * here + before).astype(BF16), (after - before).astype(BF16)


def kernel(
    width_ref, slot_ref, near_ref, lens_ref, pot_ref, out_ref,
    own, top, bot, pack, rowm, colm, coef, arrived, leaving, conv,
    load_sem, halo_send, halo_recv, state_send, state_recv, store_sem,
):
    depth, sky = lax.axis_index("depth"), lax.axis_index("sky")
    has_before, has_after = sky > 0, sky < lax.axis_size("sky") - 1
    takes, gives = depth > 0, depth < lax.axis_size("depth") - 1
    planes, rows, cols = pot_ref.shape
    ninth = pack.shape[1]
    pieces, tiles, bands = cols // LANES, cols // TILE, rows // EIGHT
    middle = pl.ds(LANES, cols)

    load = pltpu.make_async_copy(pot_ref, own.at[:, :, middle], load_sem)
    load.start()
    barrier = pltpu.get_barrier_semaphore()
    partners = (
        (has_before, {"sky": sky - 1}), (has_after, {"sky": sky + 1}),
        (takes, {"depth": depth - 1}), (gives, {"depth": depth + 1}),
    )
    for there, partner in partners:
        @pl.when(there)
        def _(partner=partner):
            pl.semaphore_signal(barrier, inc=1, device_id=partner, device_id_type=MESH)

    for buffer in (own, top, bot):
        for edge in (pl.ds(0, LANES), pl.ds(LANES + cols, LANES)):
            buffer[:, :, edge] = jnp.zeros((buffer.shape[0], buffer.shape[1], LANES), F32)
    for there, buffer in ((has_before, top), (has_after, bot)):
        @pl.when(jnp.logical_not(there))
        def _(buffer=buffer):
            buffer[...] = jnp.zeros_like(buffer)
    pack[...] = jnp.zeros_like(pack)
    load.wait()
    for side, row in ((0, rows - WMAX - 1), (1, WMAX)):
        for k in range(planes):
            pack[side, k // EIGHT, pl.ds(k % EIGHT, 1), :] = own[k, pl.ds(row, 1), middle]

    pl.semaphore_wait(barrier, sum(there.astype(jnp.int32) for there, _ in partners))

    def halo(side, part, piece):
        col = pl.multiple_of(piece * LANES, LANES)
        landing = (top, bot)[side]
        lanes_there = pl.ds(pl.multiple_of(col + LANES, LANES), LANES)
        if part == 0:
            source = pot_ref.at[:, pl.ds((rows - WMAX, 0)[side], WMAX), pl.ds(col, LANES)]
            target = landing.at[pl.ds(0, planes), :, lanes_there]
        else:
            source = pack.at[side, :, :, pl.ds(col, LANES)]
            target = landing.at[pl.ds(planes, ninth), :, lanes_there]
        return pltpu.make_async_remote_copy(
            src_ref=source, dst_ref=target,
            send_sem=halo_send.at[side, part, piece], recv_sem=halo_recv.at[side, part, piece],
            device_id={"sky": sky + (1, -1)[side]}, device_id_type=MESH,
        )

    sends, lands = (has_after, has_before), (has_before, has_after)

    def send_halo(piece, carry):
        for side in (0, 1):
            @pl.when(sends[side])
            def _(side=side):
                halo(side, 0, piece).start()
                halo(side, 1, piece).start()
        return carry

    lax.fori_loop(0, pieces, send_halo, 0)

    def await_halo(piece):
        for side in (0, 1):
            @pl.when(lands[side])
            def _(side=side):
                halo(side, 0, piece).wait_recv()
                halo(side, 1, piece).wait_recv()

    @pl.when(jnp.logical_not(takes))
    def _():
        def start(tile, carry):
            for entry in range(8):
                arrived[tile, entry] = jnp.full((EIGHT, TILE), (1.0, 0.0, 0.0, 1.0)[entry % 4], F32)
            return carry
        lax.fori_loop(0, tiles * bands, start, 0)

    own_rows = rows + 2 * WMAX
    tall = own_rows + 2 * EIGHT * ninth

    def build(k, carry):
        half_width = width_ref[k]
        place = lax.broadcasted_iota(jnp.int32, (rows, 2 * tall), 1)
        place = jnp.where(place >= tall, place - tall, place)
        far_up = jnp.where(place - own_rows == k, -WMAX - 1, FAR)
        far_down = jnp.where(place - own_rows - EIGHT * ninth == k, rows + WMAX, FAR)
        row = jnp.where(place < rows, place, jnp.where(
            place < rows + WMAX, place - rows - WMAX, jnp.where(
                place < own_rows, place - WMAX, jnp.where(
                    place < own_rows + EIGHT * ninth, far_up, far_down))))
        box, second, central = stencils(row - lax.broadcasted_iota(jnp.int32, (rows, 2 * tall), 0), half_width)
        rowm[k, 0:rows, :] = box
        rowm[k, rows:2 * rows, :] = second
        rowm[k, 2 * rows:3 * rows, :] = central
        shape = (3 * LANES, LANES)
        gap = lax.broadcasted_iota(jnp.int32, shape, 0) - lax.broadcasted_iota(jnp.int32, shape, 1) - LANES
        box, second, central = stencils(gap, half_width)
        colm[k, 0] = second
        colm[k, 1] = box
        colm[k, 2] = central
        return carry

    lax.fori_loop(0, planes, build, 0)

    def curvature(tile):
        col = pl.multiple_of(tile * TILE, TILE)
        window = pl.ds(col, TILE + 2 * LANES)

        def plane(k, carry):
            half_width = width_ref[k]
            near = near_ref[slot_ref[k]]
            lens = lens_ref[slot_ref[k]]
            share = jnp.float32(1.0 / (2 * WMAX + 1) ** 2)
            for width in range(1, WMAX):
                share = jnp.where(half_width == width, jnp.float32(1.0 / (2 * width + 1) ** 2), share)
            strength = lens * share
            values = [own[k, :, window], top[k, :, window], bot[k, :, window]]
            values += [buffer[planes + i, :, window] for buffer in (top, bot) for i in range(ninth)]
            tall_values = jnp.concatenate(split(jnp.concatenate(values, axis=0)), axis=0)
            along = jnp.dot(rowm[k], tall_values, preferred_element_type=F32)
            along_high, along_low = split(along)
            for kind in range(3):
                band = slice(kind * rows, (kind + 1) * rows)
                left, right = slice(0, 3 * LANES), slice(LANES, 4 * LANES)
                stacked = jnp.concatenate([
                    along_high[band, left], along_low[band, left],
                    along_high[band, right], along_low[band, right]], axis=0)
                both = jnp.dot(stacked, colm[k, kind], preferred_element_type=F32)
                full = jnp.concatenate([
                    both[0:rows] + both[rows:2 * rows],
                    both[2 * rows:3 * rows] + both[3 * rows:4 * rows]], axis=1)
                if kind == 2:
                    coef[k, kind, :, pl.ds(col, TILE)] = (-0.25 * strength) * full
                else:
                    coef[k, kind, :, pl.ds(col, TILE)] = near - strength * full
            return carry

        lax.fori_loop(0, planes, plane, 0)

    def state(index):
        return pltpu.make_async_remote_copy(
            src_ref=leaving.at[index], dst_ref=arrived.at[index],
            send_sem=state_send.at[index], recv_sem=state_recv.at[index],
            device_id={"depth": depth + 1}, device_id_type=MESH,
        )

    def store(tile):
        lanes = pl.ds(pl.multiple_of(tile * TILE, TILE), TILE)
        return pltpu.make_async_copy(conv.at[:, :, lanes], out_ref.at[:, :, lanes], store_sem.at[tile])

    def advance(tile):
        lanes = pl.ds(pl.multiple_of(tile * TILE, TILE), TILE)
        for band in range(bands):
            index = tile * bands + band
            band_rows = slice(band * EIGHT, (band + 1) * EIGHT)

            @pl.when(takes)
            def _(index=index):
                state(index).wait_recv()

            now = [arrived[index, entry] for entry in range(4)]
            past = [arrived[index, 4 + entry] for entry in range(4)]
            for k in range(planes):
                retained = 1.0 - near_ref[slot_ref[k]]
                xx = coef[k, 0, band_rows, lanes]
                yy = coef[k, 1, band_rows, lanes]
                xy = coef[k, 2, band_rows, lanes]
                ahead = [
                    xx * now[0] + xy * now[2] + retained * past[0],
                    xx * now[1] + xy * now[3] + retained * past[1],
                    xy * now[0] + yy * now[2] + retained * past[2],
                    xy * now[1] + yy * now[3] + retained * past[3],
                ]
                now, past = ahead, now
                conv[k, band_rows, lanes] = 1.0 - 0.5 * (ahead[0] + ahead[3])
            for entry in range(4):
                leaving[index, entry] = now[entry]
                leaving[index, 4 + entry] = past[entry]

            @pl.when(gives)
            def _(index=index):
                state(index).start()

        store(tile).start()

    await_halo(0)

    def step(tile, carry):
        await_halo(2 * tile + 1)

        @pl.when(tile < tiles - 1)
        def _():
            await_halo(2 * tile + 2)

        curvature(tile)
        advance(tile)
        return carry

    lax.fori_loop(0, tiles, step, 0)

    def finish_halo(piece, carry):
        for side in (0, 1):
            @pl.when(sends[side])
            def _(side=side):
                halo(side, 0, piece).wait_send()
                halo(side, 1, piece).wait_send()
        return carry

    lax.fori_loop(0, pieces, finish_halo, 0)

    @pl.when(gives)
    def _():
        def finish(index, carry):
            state(index).wait_send()
            return carry
        lax.fori_loop(0, tiles * bands, finish, 0)

    def finish_store(tile, carry):
        store(tile).wait()
        return carry

    lax.fori_loop(0, tiles, finish_store, 0)


def per_device(potential, widths, plane_slot, ratio_near, ratio_lens):
    planes, rows, cols = potential.shape
    ninth = round_up(planes, EIGHT) // EIGHT
    wide = cols + 2 * LANES
    tall = rows + 2 * WMAX + 2 * EIGHT * ninth
    states = (cols // TILE) * (rows // EIGHT)
    smem = pl.BlockSpec(memory_space=pltpu.SMEM)
    return pl.pallas_call(
        kernel,
        out_shape=jax.ShapeDtypeStruct(potential.shape, F32),
        in_specs=[smem, smem, smem, smem, pl.BlockSpec(memory_space=pl.ANY)],
        out_specs=pl.BlockSpec(memory_space=pl.ANY),
        scratch_shapes=[
            pltpu.VMEM((planes, rows, wide), F32),
            pltpu.VMEM((planes + ninth, EIGHT, wide), F32),
            pltpu.VMEM((planes + ninth, EIGHT, wide), F32),
            pltpu.VMEM((2, ninth, EIGHT, cols), F32),
            pltpu.VMEM((planes, 3 * rows, 2 * tall), BF16),
            pltpu.VMEM((planes, 3, 3 * LANES, LANES), BF16),
            pltpu.VMEM((planes, 3, rows, cols), F32),
            pltpu.VMEM((states, 8, EIGHT, TILE), F32),
            pltpu.VMEM((states, 8, EIGHT, TILE), F32),
            pltpu.VMEM((planes, rows, cols), F32),
            pltpu.SemaphoreType.DMA,
            pltpu.SemaphoreType.DMA((2, 2, cols // LANES)),
            pltpu.SemaphoreType.DMA((2, 2, cols // LANES)),
            pltpu.SemaphoreType.DMA((states,)),
            pltpu.SemaphoreType.DMA((states,)),
            pltpu.SemaphoreType.DMA((cols // TILE,)),
        ],
        compiler_params=pltpu.CompilerParams(collective_id=0, has_side_effects=True),
        name="lensing",
    )(widths, plane_slot, ratio_near, ratio_lens, potential)


def solution(mesh):
    return jax.shard_map(
        per_device,
        mesh=mesh,
        in_specs=(P("depth", "sky", None), P("depth"), P("depth"), P(), P()),
        out_specs=P("depth", "sky", None),
        check_vma=False,
    )
```

time: 1140 us -> 118 us (0.10); the launches traced: 1130 us -> 118 us
  other arithmetic: 502 us -> 0 us
  loops' own time: 242 us -> 0 us
  local copies, waits for them, and re-layouts: 226 us -> 3.91 us
  waiting for transfers between devices: 134 us -> 0 us
  Pallas kernels: 0 us -> 114 us
  starting transfers between devices: 22 us -> 0 us
    mul x396 -> x0, other arithmetic: 326 us -> none  [the longest x264 169 us: advance(): row_first = entry_xx * upper[0] + entry_xy * upper[1] + retained * lower[0]]
    another operation x13 -> x0, loops' own time: 242 us -> none  [the longest x11 163 us: propagate(): lax.scan(plane, carried, (curvatures[0], curvatures[1], curvatures[2], ne...]
    dynamic_slice x298 -> x0, local copies, waits for them, and re-layouts: 194 us -> none  [the longest x264 157 us: propagate(): lax.scan(plane, carried, (curvatures[0], curvatures[1], curvatures[2], ne...]
    ppermute x13 -> x0, waiting for transfers between devices: 134 us -> none  [the longest x11 106 us: passed_along(): lax.ppermute(value, axis, [(source, source + steps) for source in range(f...]
    dynamic_update_slice x155 -> x0, other arithmetic: 129 us -> none  [the longest x132 88.8 us: propagate(): lax.scan(plane, carried, (curvatures[0], curvatures[1], curvatures[2], ne...]
    pallas_call x0 -> x1, Pallas kernels: none -> 114 us  [per_device(): pl.pallas_call(kernel, out_shape=jax.ShapeDtypeStruct(potential.shape, F3...]
    div x24 -> x0, other arithmetic: 37.6 us -> none  [box_filter(): return summed / (2.0 * half_width.astype(jnp.float32) + 1.0)]
    ppermute x13 -> x0, starting transfers between devices: 22 us -> none  [the longest x11 14.1 us: passed_along(): lax.ppermute(value, axis, [(source, source + steps) for source in range(f...]
  transfers between devices with their start and end apart: 13 -> 0, of which waited for: 13 -> 0; matrix products, arithmetic and copies ran while one was open for 3% -> 0% of each run, Pallas kernels for 0% -> 0%
where the time goes in v1:
time: 118 us
  Pallas kernels  114 us (97%)
  local copies, waits for them, and re-layouts  3.91 us (3%)
    pallas_call x1, Pallas kernels, per_device(): pl.pallas_call(kernel, out_shape=jax.ShapeDtypeStruct(potential.shape, F3...  114 us
    unnamed x1, local copies, waits for them, and re-layouts  3.91 us

profile of v1, /device:TPU:119, one launch (start us, length us, event | category | flops | bytes accessed | tf_op | source)
XLA Modules:
  0.0 118.0 jit_solution(18328574116797701344)
XLA Ops:
  0.0 114.1 %lensing.1 = f32[12,32,2048]{2,1,0:T(8,128)} custom-call(s32[12]{0:T(128)} %width_ref.1, s32[12]{0:T(128)} %slot_ref.1, f32[16]{0:T(128)} %near_ref.1, f32[16]{0:T(128)} %lens_ref.1, f32[12,32,2048]{2,1,0:T(8,128)} %pot_ref.1), custom_call_target="tpu_custom_call" | custom-call | tf_op jit(solution)/shard_map/lensing/pallas_call | solution.py:270
  114.1 3.9 %copy.7 = f32[12,32,2048]{2,1,0:T(8,128)} copy(f32[12,32,2048]{2,1,0:T(8,128)} %lensing.1) | data formatting | bytes 6291456

commit v2 on v1

v2 whole, which is shorter than its diff:
```python
import jax
import jax.numpy as jnp
from jax import lax
from jax.experimental import pallas as pl
from jax.experimental.pallas import tpu as pltpu
from jax.sharding import PartitionSpec as P

WMAX = 8
LANES = 128
EIGHT = 8
TILE = 256
UNROLL = 6
SPAN = 128
FAR = 1000
MESH = pl.DeviceIdType.MESH
F32 = jnp.float32
BF16 = jnp.bfloat16


def round_up(value, step):
    return -(-value // step) * step


def split(values):
    high = values.astype(BF16)
    return high, (values - high.astype(F32)).astype(BF16)


def inside(distance, half_width):
    return jnp.where(jnp.abs(distance) <= half_width, 1.0, 0.0)


def kernel(
    width_ref, slot_ref, near_ref, lens_ref, pot_ref, out_ref,
    own, top, bot, pack, nears, strengths, rowm, colm, along, coef, arrived, leaving,
    load_sem, halo_send, halo_recv, state_send, state_recv,
):
    depth, sky = lax.axis_index("depth"), lax.axis_index("sky")
    has_before, has_after = sky > 0, sky < lax.axis_size("sky") - 1
    takes, gives = depth > 0, depth < lax.axis_size("depth") - 1
    planes, rows, cols = pot_ref.shape
    ninth = pack.shape[1]
    pieces, tiles, parts = cols // LANES, cols // TILE, TILE // SPAN
    units = parts * (rows // EIGHT)
    middle = pl.ds(LANES, cols)

    load = pltpu.make_async_copy(pot_ref, own.at[:, :, middle], load_sem)
    load.start()
    barrier = pltpu.get_barrier_semaphore()
    partners = (
        (has_before, {"sky": sky - 1}), (has_after, {"sky": sky + 1}),
        (takes, {"depth": depth - 1}), (gives, {"depth": depth + 1}),
    )
    for there, partner in partners:
        @pl.when(there)
        def _(partner=partner):
            pl.semaphore_signal(barrier, inc=1, device_id=partner, device_id_type=MESH)

    for buffer in (own, top, bot):
        for edge in (pl.ds(0, LANES), pl.ds(LANES + cols, LANES)):
            buffer[:, :, edge] = jnp.zeros((buffer.shape[0], buffer.shape[1], LANES), F32)
    for there, buffer in ((has_before, top), (has_after, bot)):
        @pl.when(jnp.logical_not(there))
        def _(buffer=buffer):
            buffer[...] = jnp.zeros_like(buffer)
    pack[...] = jnp.zeros_like(pack)
    load.wait()
    for side, row in ((0, rows - WMAX - 1), (1, WMAX)):
        for k in range(planes):
            pack[side, k // EIGHT, pl.ds(k % EIGHT, 1), :] = own[k, pl.ds(row, 1), middle]

    pl.semaphore_wait(barrier, sum(there.astype(jnp.int32) for there, _ in partners))

    def halo(side, part, piece):
        col = pl.multiple_of(piece * LANES, LANES)
        landing = (top, bot)[side]
        lanes_there = pl.ds(pl.multiple_of(col + LANES, LANES), LANES)
        if part == 0:
            source = pot_ref.at[:, pl.ds((rows - WMAX, 0)[side], WMAX), pl.ds(col, LANES)]
            target = landing.at[pl.ds(0, planes), :, lanes_there]
        else:
            source = pack.at[side, :, :, pl.ds(col, LANES)]
            target = landing.at[pl.ds(planes, ninth), :, lanes_there]
        return pltpu.make_async_remote_copy(
            src_ref=source, dst_ref=target,
            send_sem=halo_send.at[side, part, piece], recv_sem=halo_recv.at[side, part, piece],
            device_id={"sky": sky + (1, -1)[side]}, device_id_type=MESH,
        )

    sends, lands = (has_after, has_before), (has_before, has_after)

    def send_halo(piece, carry):
        for side in (0, 1):
            @pl.when(sends[side])
            def _(side=side):
                halo(side, 0, piece).start()
                halo(side, 1, piece).start()
        return carry

    lax.fori_loop(0, pieces, send_halo, 0)

    def await_halo(piece):
        for side in (0, 1):
            @pl.when(lands[side])
            def _(side=side):
                halo(side, 0, piece).wait_recv()
                halo(side, 1, piece).wait_recv()

    @pl.when(jnp.logical_not(takes))
    def _():
        def start(tile, carry):
            for entry in range(8):
                arrived[tile, entry] = jnp.full((EIGHT, SPAN), (1.0, 0.0, 0.0, 1.0)[entry % 4], F32)
            return carry
        lax.fori_loop(0, tiles * units, start, 0)

    own_rows = rows + 2 * WMAX
    tall = own_rows + 2 * EIGHT * ninth

    def build(k, carry):
        half_width = width_ref[k]
        share = jnp.float32(1.0 / (2 * WMAX + 1) ** 2)
        for width in range(1, WMAX):
            share = jnp.where(half_width == width, jnp.float32(1.0 / (2 * width + 1) ** 2), share)
        nears[k] = near_ref[slot_ref[k]]
        strengths[k] = lens_ref[slot_ref[k]] * share
        place = lax.broadcasted_iota(jnp.int32, (rows, 2 * tall), 1)
        place = jnp.where(place >= tall, place - tall, place)
        far_up = jnp.where(place - own_rows == k, -WMAX - 1, FAR)
        far_down = jnp.where(place - own_rows - EIGHT * ninth == k, rows + WMAX, FAR)
        row = jnp.where(place < rows, place, jnp.where(
            place < rows + WMAX, place - rows - WMAX, jnp.where(
                place < own_rows, place - WMAX, jnp.where(
                    place < own_rows + EIGHT * ninth, far_up, far_down))))
        distance = row - lax.broadcasted_iota(jnp.int32, (rows, 2 * tall), 0)
        after, here, before = (inside(distance + shift, half_width) for shift in (-1, 0, 1))
        rowm[k, 0:rows, :] = here.astype(BF16)
        rowm[k, rows:2 * rows, :] = (after - before).astype(BF16)
        rowm[k, 2 * rows:3 * rows, :] = (after - 2.0 * here + before).astype(BF16)
        shape = (2 * LANES, LANES)
        gap = lax.broadcasted_iota(jnp.int32, shape, 0) - lax.broadcasted_iota(jnp.int32, shape, 1)
        colm[k] = inside(gap - LANES // 2, half_width).astype(BF16)
        return carry

    lax.fori_loop(0, planes, build, 0)

    def along_rows(chunk):
        window = pl.ds(pl.multiple_of(chunk * TILE, TILE), TILE)

        def plane(k, carry):
            values = [own[k, :, window], top[k, :, window], bot[k, :, window]]
            values += [buffer[planes + i, :, window] for buffer in (top, bot) for i in range(ninth)]
            terms = jnp.concatenate(split(jnp.concatenate(values, axis=0)), axis=0)
            along[k, :, window] = jnp.dot(rowm[k], terms, preferred_element_type=F32)
            return carry

        lax.fori_loop(0, planes, plane, 0, unroll=UNROLL)

    def along_columns(tile):
        col = pl.multiple_of(tile * TILE, TILE)
        lane = lax.broadcasted_iota(jnp.int32, (rows, LANES), 1)

        def plane(k, carry):
            half_width, near, strength = width_ref[k], nears[k], strengths[k]

            def blocks(kind):
                return [along[k, kind * rows:(kind + 1) * rows, pl.ds(pl.multiple_of(col + i * LANES, LANES), LANES)]
                        for i in range(4)]

            def spread(values):
                turned = [pltpu.roll(value, LANES - half_width, 1) for value in values[1:]]
                ahead = [jnp.where(lane < LANES - half_width, turned[i], turned[i + 1]) for i in range(2)]
                turned = [pltpu.roll(value, half_width + 1, 1) for value in values[:-1]]
                behind = [jnp.where(lane > half_width, turned[i + 1], turned[i]) for i in range(2)]
                return jnp.concatenate([ahead[i] - behind[i] for i in range(2)], axis=1)

            def neighbours(values):
                turned = [pltpu.roll(value, LANES - 1, 1) for value in values]
                return [jnp.where(lane < LANES - 1, turned[i], turned[i + 1]) for i in range(3)] + turned[3:]

            boxed = blocks(0)
            xx = spread([after - here for after, here in zip(neighbours(boxed), boxed)])
            coef[k, 0, :, pl.ds(col, TILE)] = near - strength * xx
            slopes = blocks(1)
            xy = spread([after + here for after, here in zip(neighbours(slopes), slopes)])
            coef[k, 2, :, pl.ds(col, TILE)] = (-0.25 * strength) * xy
            turned = [pltpu.roll(value, LANES // 2, 1) for value in blocks(2)]
            halves = [jnp.where(lane < LANES // 2, turned[i], turned[i + 1]) for i in range(3)]
            terms = [split(half) for half in halves]
            stacked = jnp.concatenate([
                jnp.concatenate([terms[i][term], terms[i + 1][term]], axis=1)
                for i in range(2) for term in range(2)], axis=0)
            both = jnp.dot(stacked, colm[k], preferred_element_type=F32)
            yy = jnp.concatenate([
                both[2 * i * rows:(2 * i + 1) * rows] + both[(2 * i + 1) * rows:(2 * i + 2) * rows]
                for i in range(2)], axis=1)
            coef[k, 1, :, pl.ds(col, TILE)] = near - strength * yy
            return carry

        lax.fori_loop(0, planes, plane, 0, unroll=UNROLL)

    def state(index):
        return pltpu.make_async_remote_copy(
            src_ref=leaving.at[index], dst_ref=arrived.at[index],
            send_sem=state_send.at[index], recv_sem=state_recv.at[index],
            device_id={"depth": depth + 1}, device_id_type=MESH,
        )

    def advance(tile):
        for unit in range(units):
            index = tile * units + unit
            band, part = unit // parts, unit % parts
            band_rows = slice(band * EIGHT, (band + 1) * EIGHT)
            lanes = pl.ds(pl.multiple_of(tile * TILE + part * SPAN, SPAN), SPAN)

            @pl.when(takes)
            def _(index=index):
                state(index).wait_recv()

            now = [arrived[index, entry] for entry in range(4)]
            past = [arrived[index, 4 + entry] for entry in range(4)]
            for k in range(planes):
                retained = 1.0 - nears[k]
                xx = coef[k, 0, band_rows, lanes]
                yy = coef[k, 1, band_rows, lanes]
                xy = coef[k, 2, band_rows, lanes]
                ahead = [
                    xx * now[0] + xy * now[2] + retained * past[0],
                    xx * now[1] + xy * now[3] + retained * past[1],
                    xy * now[0] + yy * now[2] + retained * past[2],
                    xy * now[1] + yy * now[3] + retained * past[3],
                ]
                now, past = ahead, now
                out_ref[k, band_rows, lanes] = 1.0 - 0.5 * (ahead[0] + ahead[3])
            for entry in range(4):
                leaving[index, entry] = now[entry]
                leaving[index, 4 + entry] = past[entry]

            @pl.when(gives)
            def _(index=index):
                state(index).start()

    await_halo(0)
    along_rows(0)
    lead = jnp.minimum(2 * depth, tiles)

    def step(turn, carry):
        @pl.when(turn < tiles)
        def _():
            await_halo(2 * turn + 1)

            @pl.when(turn < tiles - 1)
            def _():
                await_halo(2 * turn + 2)

            along_rows(turn + 1)
            along_columns(turn)

        @pl.when((turn >= lead) & (turn - lead < tiles))
        def _():
            advance(turn - lead)

        return carry

    lax.fori_loop(0, tiles + lead, step, 0)

    def finish_halo(piece, carry):
        for side in (0, 1):
            @pl.when(sends[side])
            def _(side=side):
                halo(side, 0, piece).wait_send()
                halo(side, 1, piece).wait_send()
        return carry

    lax.fori_loop(0, pieces, finish_halo, 0)

    @pl.when(gives)
    def _():
        def finish(index, carry):
            state(index).wait_send()
            return carry
        lax.fori_loop(0, tiles * units, finish, 0)


def per_device(potential, widths, plane_slot, ratio_near, ratio_lens):
    planes, rows, cols = potential.shape
    ninth = round_up(planes, EIGHT) // EIGHT
    wide = cols + 2 * LANES
    tall = rows + 2 * WMAX + 2 * EIGHT * ninth
    states = (cols // SPAN) * (rows // EIGHT)
    smem = pl.BlockSpec(memory_space=pltpu.SMEM)
    return pl.pallas_call(
        kernel,
        out_shape=pltpu.VMEM(potential.shape, F32),
        in_specs=[smem, smem, smem, smem, pl.BlockSpec(memory_space=pl.ANY)],
        out_specs=pl.BlockSpec(memory_space=pltpu.VMEM),
        scratch_shapes=[
            pltpu.VMEM((planes, rows, wide), F32),
            pltpu.VMEM((planes + ninth, EIGHT, wide), F32),
            pltpu.VMEM((planes + ninth, EIGHT, wide), F32),
            pltpu.VMEM((2, ninth, EIGHT, cols), F32),
            pltpu.SMEM((planes,), F32),
            pltpu.SMEM((planes,), F32),
            pltpu.VMEM((planes, 3 * rows, 2 * tall), BF16),
            pltpu.VMEM((planes, 2 * LANES, LANES), BF16),
            pltpu.VMEM((planes, 3 * rows, wide), F32),
            pltpu.VMEM((planes, 3, rows, cols), F32),
            pltpu.VMEM((states, 8, EIGHT, SPAN), F32),
            pltpu.VMEM((states, 8, EIGHT, SPAN), F32),
            pltpu.SemaphoreType.DMA,
            pltpu.SemaphoreType.DMA((2, 2, cols // LANES)),
            pltpu.SemaphoreType.DMA((2, 2, cols // LANES)),
            pltpu.SemaphoreType.DMA((states,)),
            pltpu.SemaphoreType.DMA((states,)),
        ],
        compiler_params=pltpu.CompilerParams(
            collective_id=0, has_side_effects=True, vmem_limit_bytes=48 * 2**20),
        name="lensing",
    )(*(pltpu.with_memory_space_constraint(table, pltpu.HBM) for table in (widths, plane_slot, ratio_near, ratio_lens)), potential)


def solution(mesh):
    return jax.shard_map(
        per_device,
        mesh=mesh,
        in_specs=(P("depth", "sky", None), P("depth"), P("depth"), P(), P()),
        out_specs=P("depth", "sky", None),
        check_vma=False,
    )
```

time: 118 us -> 98 us (0.83); the launches traced: 118 us -> 96.4 us
  Pallas kernels: 114 us -> 94.7 us
  local copies, waits for them, and re-layouts: 3.91 us -> 1.67 us
    pallas_call x1, Pallas kernels: 114 us -> 94.7 us  [per_device(): pl.pallas_call(kernel, out_shape=pltpu.VMEM(potential.shape, F32), in_spe...]
    unnamed x1, local copies, waits for them, and re-layouts: 3.91 us -> 1.67 us
where the time goes in v2:
time: 98 us; the launch traced here: 96.4 us
  Pallas kernels  94.7 us (97%)
  local copies, waits for them, and re-layouts  1.67 us (2%)
    pallas_call x1, Pallas kernels, per_device(): pl.pallas_call(kernel, out_shape=pltpu.VMEM(potential.shape, F32), in_spe...  94.7 us

profile of v2, /device:TPU:119, one launch (start us, length us, event | category | flops | bytes accessed | tf_op | source)
XLA Modules:
  0.0 96.4 jit_solution(17191081035961161985)
XLA Ops:
  0.0 94.7 %lensing.1 = f32[12,32,2048]{2,1,0:T(8,128)S(1)} custom-call(s32[12]{0:T(128)} %width_ref.1, s32[12]{0:T(128)} %slot_ref.1, f32[16]{0:T(128)} %near_ref.1, f32[16]{0:T(128)} %lens_ref.1, f32[12,32,2048]{2,1,0:T(8,128)} %pot_ref.1), custom_call_target="tpu_custom_call" | custom-call | tf_op jit(solution)/shard_map/lensing/pallas_call | solution.py:292
  94.7 1.7 %copy.7 = f32[12,32,2048]{2,1,0:T(8,128)} copy(f32[12,32,2048]{2,1,0:T(8,128)S(1)} %lensing.1) | data formatting | bytes 6291456

commit v3 on v2

--- a/solution.py
+++ b/solution.py
@@ -9,9 +9,10 @@
 LANES = 128
 EIGHT = 8
 TILE = 256
-UNROLL = 6
 SPAN = 128
 FAR = 1000
+PAIR = 2
+DETOUR = (2, 4)
 MESH = pl.DeviceIdType.MESH
 F32 = jnp.float32
 BF16 = jnp.bfloat16
@@ -32,8 +33,8 @@
 
 def kernel(
     width_ref, slot_ref, near_ref, lens_ref, pot_ref, out_ref,
-    own, top, bot, pack, nears, strengths, rowm, colm, along, coef, arrived, leaving,
-    load_sem, halo_send, halo_recv, state_send, state_recv,
+    own, top, bot, pack, relay, nears, strengths, rowm, colm, along, coef, arrived, leaving,
+    load_sem, halo_send, halo_recv, relay_send, relay_recv, forward_send, state_send, state_recv,
 ):
     depth, sky = lax.axis_index("depth"), lax.axis_index("sky")
     has_before, has_after = sky > 0, sky < lax.axis_size("sky") - 1
@@ -41,13 +42,28 @@
     planes, rows, cols = pot_ref.shape
     ninth = pack.shape[1]
     pieces, tiles, parts = cols // LANES, cols // TILE, TILE // SPAN
-    units = parts * (rows // EIGHT)
+    bands = rows // EIGHT
+    units = parts * bands
     middle = pl.ds(LANES, cols)
 
     load = pltpu.make_async_copy(pot_ref, own.at[:, :, middle], load_sem)
     load.start()
+    x, x_size = depth // PAIR, lax.axis_size("depth") // PAIR
+    mirror = depth + PAIR * (x_size - 1 - 2 * x)
+    detours, relays = x < x_size // 2, x >= x_size - x_size // 2
+    at_end = (x == 0) | (x == x_size - 1)
+    detoured = jnp.where(at_end, pieces // DETOUR[0], pieces // DETOUR[1])
+    first = pieces - detoured
+    odd = sky % 2 == 1
+    leaves = (odd & has_after, jnp.logical_not(odd) & has_before)
+    enters = (jnp.logical_not(odd) & has_before, odd & has_after)
+    outside = leaves[0] | leaves[1]
+
     barrier = pltpu.get_barrier_semaphore()
     partners = (
+        ((detours | relays) & outside, {"depth": mirror}),
+        ((detours | relays) & leaves[0], {"depth": mirror, "sky": sky + 1}),
+        ((detours | relays) & leaves[1], {"depth": mirror, "sky": sky - 1}),
         (has_before, {"sky": sky - 1}), (has_after, {"sky": sky + 1}),
         (takes, {"depth": depth - 1}), (gives, {"depth": depth + 1}),
     )
@@ -89,19 +105,69 @@
 
     sends, lands = (has_after, has_before), (has_before, has_after)
 
-    def send_halo(piece, carry):
+    def by_mirror(side, part, index):
+        col = pl.multiple_of((first + index) * LANES, LANES)
+        if part == 0:
+            source = pot_ref.at[:, pl.ds((rows - WMAX, 0)[side], WMAX), pl.ds(col, LANES)]
+            target = relay.at[index, pl.ds(0, planes)]
+        else:
+            source = pack.at[side, :, :, pl.ds(col, LANES)]
+            target = relay.at[index, pl.ds(planes, ninth)]
+        return pltpu.make_async_remote_copy(
+            src_ref=source, dst_ref=target,
+            send_sem=relay_send.at[part, index], recv_sem=relay_recv.at[part, index],
+            device_id={"depth": mirror}, device_id_type=MESH,
+        )
+
+    def forward(side, index):
+        piece = first + index
+        lanes_there = pl.ds(pl.multiple_of(piece * LANES + LANES, LANES), LANES)
+        return pltpu.make_async_remote_copy(
+            src_ref=relay.at[index], dst_ref=(top, bot)[side].at[:, :, lanes_there],
+            send_sem=forward_send.at[index], recv_sem=halo_recv.at[side, 0, piece],
+            device_id={"depth": mirror, "sky": sky + (1, -1)[side]}, device_id_type=MESH,
+        )
+
+    def each_detoured(act):
         for side in (0, 1):
-            @pl.when(sends[side])
+            @pl.when(detours & leaves[side])
             def _(side=side):
-                halo(side, 0, piece).start()
-                halo(side, 1, piece).start()
-        return carry
-
-    lax.fori_loop(0, pieces, send_halo, 0)
+                def one(index, carry):
+                    act(by_mirror(side, 0, index))
+                    act(by_mirror(side, 1, index))
+                    return carry
+                lax.fori_loop(0, detoured, one, 0)
+
+    def each_direct(act):
+        def one(piece, carry):
+            for side in (0, 1):
+                @pl.when(sends[side] & jnp.logical_not(detours & leaves[side] & (piece >= first)))
+                def _(side=side):
+                    act(halo(side, 0, piece))
+                    act(halo(side, 1, piece))
+            return carry
+        lax.fori_loop(0, pieces, one, 0)
+
+    each_detoured(lambda copy: copy.start())
+    each_direct(lambda copy: copy.start())
+
+    def pass_on(index):
+        for side in (0, 1):
+            @pl.when(relays & leaves[side] & (index < detoured))
+            def _(side=side):
+                by_mirror(side, 0, index).wait_recv()
+                by_mirror(side, 1, index).wait_recv()
+                forward(side, index).start()
 
     def await_halo(piece):
         for side in (0, 1):
-            @pl.when(lands[side])
+            turned = detours & enters[side] & (piece >= first)
+
+            @pl.when(lands[side] & turned)
+            def _(side=side):
+                forward(side, piece - first).wait_recv()
+
+            @pl.when(lands[side] & jnp.logical_not(turned))
             def _(side=side):
                 halo(side, 0, piece).wait_recv()
                 halo(side, 1, piece).wait_recv()
@@ -144,60 +210,51 @@
 
     lax.fori_loop(0, planes, build, 0)
 
-    def along_rows(chunk):
+    def along_rows(chunk, k):
         window = pl.ds(pl.multiple_of(chunk * TILE, TILE), TILE)
-
-        def plane(k, carry):
-            values = [own[k, :, window], top[k, :, window], bot[k, :, window]]
-            values += [buffer[planes + i, :, window] for buffer in (top, bot) for i in range(ninth)]
-            terms = jnp.concatenate(split(jnp.concatenate(values, axis=0)), axis=0)
-            along[k, :, window] = jnp.dot(rowm[k], terms, preferred_element_type=F32)
-            return carry
-
-        lax.fori_loop(0, planes, plane, 0, unroll=UNROLL)
-
-    def along_columns(tile):
+        values = [own[k, :, window], top[k, :, window], bot[k, :, window]]
+        values += [buffer[planes + i, :, window] for buffer in (top, bot) for i in range(ninth)]
+        terms = jnp.concatenate(split(jnp.concatenate(values, axis=0)), axis=0)
+        along[k, :, window] = jnp.dot(rowm[k], terms, preferred_element_type=F32)
+
+    def along_columns(tile, k):
         col = pl.multiple_of(tile * TILE, TILE)
         lane = lax.broadcasted_iota(jnp.int32, (rows, LANES), 1)
 
-        def plane(k, carry):
-            half_width, near, strength = width_ref[k], nears[k], strengths[k]
-
-            def blocks(kind):
-                return [along[k, kind * rows:(kind + 1) * rows, pl.ds(pl.multiple_of(col + i * LANES, LANES), LANES)]
-                        for i in range(4)]
-
-            def spread(values):
-                turned = [pltpu.roll(value, LANES - half_width, 1) for value in values[1:]]
-                ahead = [jnp.where(lane < LANES - half_width, turned[i], turned[i + 1]) for i in range(2)]
-                turned = [pltpu.roll(value, half_width + 1, 1) for value in values[:-1]]
-                behind = [jnp.where(lane > half_width, turned[i + 1], turned[i]) for i in range(2)]
-                return jnp.concatenate([ahead[i] - behind[i] for i in range(2)], axis=1)
-
-            def neighbours(values):
-                turned = [pltpu.roll(value, LANES - 1, 1) for value in values]
-                return [jnp.where(lane < LANES - 1, turned[i], turned[i + 1]) for i in range(3)] + turned[3:]
-
-            boxed = blocks(0)
-            xx = spread([after - here for after, here in zip(neighbours(boxed), boxed)])
-            coef[k, 0, :, pl.ds(col, TILE)] = near - strength * xx
-            slopes = blocks(1)
-            xy = spread([after + here for after, here in zip(neighbours(slopes), slopes)])
-            coef[k, 2, :, pl.ds(col, TILE)] = (-0.25 * strength) * xy
-            turned = [pltpu.roll(value, LANES // 2, 1) for value in blocks(2)]
-            halves = [jnp.where(lane < LANES // 2, turned[i], turned[i + 1]) for i in range(3)]
-            terms = [split(half) for half in halves]
-            stacked = jnp.concatenate([
-                jnp.concatenate([terms[i][term], terms[i + 1][term]], axis=1)
-                for i in range(2) for term in range(2)], axis=0)
-            both = jnp.dot(stacked, colm[k], preferred_element_type=F32)
-            yy = jnp.concatenate([
-                both[2 * i * rows:(2 * i + 1) * rows] + both[(2 * i + 1) * rows:(2 * i + 2) * rows]
-                for i in range(2)], axis=1)
-            coef[k, 1, :, pl.ds(col, TILE)] = near - strength * yy
-            return carry
-
-        lax.fori_loop(0, planes, plane, 0, unroll=UNROLL)
+        half_width, near, strength = width_ref[k], nears[k], strengths[k]
+
+        def blocks(kind):
+            return [along[k, kind * rows:(kind + 1) * rows, pl.ds(pl.multiple_of(col + i * LANES, LANES), LANES)]
+                    for i in range(4)]
+
+        def spread(values):
+            turned = [pltpu.roll(value, LANES - half_width, 1) for value in values[1:]]
+            ahead = [jnp.where(lane < LANES - half_width, turned[i], turned[i + 1]) for i in range(2)]
+            turned = [pltpu.roll(value, half_width + 1, 1) for value in values[:-1]]
+            behind = [jnp.where(lane > half_width, turned[i + 1], turned[i]) for i in range(2)]
+            return jnp.concatenate([ahead[i] - behind[i] for i in range(2)], axis=1)
+
+        def neighbours(values):
+            turned = [pltpu.roll(value, LANES - 1, 1) for value in values]
+            return [jnp.where(lane < LANES - 1, turned[i], turned[i + 1]) for i in range(3)] + turned[3:]
+
+        boxed = blocks(0)
+        xx = spread([after - here for after, here in zip(neighbours(boxed), boxed)])
+        coef[k, 0, :, pl.ds(col, TILE)] = near - strength * xx
+        slopes = blocks(1)
+        xy = spread([after + here for after, here in zip(neighbours(slopes), slopes)])
+        coef[k, 2, :, pl.ds(col, TILE)] = (-0.25 * strength) * xy
+        turned = [pltpu.roll(value, LANES // 2, 1) for value in blocks(2)]
+        halves = [jnp.where(lane < LANES // 2, turned[i], turned[i + 1]) for i in range(3)]
+        terms = [split(half) for half in halves]
+        stacked = jnp.concatenate([
+            jnp.concatenate([terms[i][term], terms[i + 1][term]], axis=1)
+            for i in range(2) for term in range(2)], axis=0)
+        both = jnp.dot(stacked, colm[k], preferred_element_type=F32)
+        yy = jnp.concatenate([
+            both[2 * i * rows:(2 * i + 1) * rows] + both[(2 * i + 1) * rows:(2 * i + 2) * rows]
+            for i in range(2)], axis=1)
+        coef[k, 1, :, pl.ds(col, TILE)] = near - strength * yy
 
     def state(index):
         return pltpu.make_async_remote_copy(
@@ -206,11 +263,10 @@
             device_id={"depth": depth + 1}, device_id_type=MESH,
         )
 
-    def advance(tile):
-        for unit in range(units):
-            index = tile * units + unit
-            band, part = unit // parts, unit % parts
-            band_rows = slice(band * EIGHT, (band + 1) * EIGHT)
+    def advance(tile, band):
+        for part in range(parts):
+            index = tile * units + band * parts + part
+            band_rows = pl.ds(pl.multiple_of(band * EIGHT, EIGHT), EIGHT)
             lanes = pl.ds(pl.multiple_of(tile * TILE + part * SPAN, SPAN), SPAN)
 
             @pl.when(takes)
@@ -241,11 +297,18 @@
                 state(index).start()
 
     await_halo(0)
-    along_rows(0)
-    lead = jnp.minimum(2 * depth, tiles)
+
+    def rows_first(k, carry):
+        along_rows(0, k)
+        return carry
+
+    lax.fori_loop(0, planes, rows_first, 0, unroll=4)
+    lead = jnp.clip(depth, 1, tiles)
 
     def step(turn, carry):
-        @pl.when(turn < tiles)
+        builds, moves = turn < tiles, turn >= lead
+
+        @pl.when(builds)
         def _():
             await_halo(2 * turn + 1)
 
@@ -253,26 +316,40 @@
             def _():
                 await_halo(2 * turn + 2)
 
-            along_rows(turn + 1)
-            along_columns(turn)
-
-        @pl.when((turn >= lead) & (turn - lead < tiles))
+        def share(band, carry):
+            @pl.when(moves)
+            def _():
+                advance(turn - lead, band)
+
+            @pl.when(builds)
+            def _():
+                group = range(planes // bands)
+                for i in group:
+                    along_rows(turn + 1, band * len(group) + i)
+                for i in group:
+                    along_columns(turn, band * len(group) + i)
+
+            return carry
+
+        lax.fori_loop(0, bands, share, 0)
+
+        @pl.when(builds)
         def _():
-            advance(turn - lead)
+            pass_on(turn)
 
         return carry
 
     lax.fori_loop(0, tiles + lead, step, 0)
 
-    def finish_halo(piece, carry):
-        for side in (0, 1):
-            @pl.when(sends[side])
-            def _(side=side):
-                halo(side, 0, piece).wait_send()
-                halo(side, 1, piece).wait_send()
-        return carry
-
-    lax.fori_loop(0, pieces, finish_halo, 0)
+    each_detoured(lambda copy: copy.wait_send())
+    each_direct(lambda copy: copy.wait_send())
+
+    @pl.when(relays & outside)
+    def _():
+        def finish(index, carry):
+            forward(0, index).wait_send()
+            return carry
+        lax.fori_loop(0, detoured, finish, 0)
 
     @pl.when(gives)
     def _():
@@ -299,6 +376,7 @@
             pltpu.VMEM((planes + ninth, EIGHT, wide), F32),
             pltpu.VMEM((planes + ninth, EIGHT, wide), F32),
             pltpu.VMEM((2, ninth, EIGHT, cols), F32),
+            pltpu.VMEM((max(1, cols // LANES // DETOUR[0]), planes + ninth, EIGHT, LANES), F32),
             pltpu.SMEM((planes,), F32),
             pltpu.SMEM((planes,), F32),
             pltpu.VMEM((planes, 3 * rows, 2 * tall), BF16),
@@ -310,6 +388,9 @@
             pltpu.SemaphoreType.DMA,
             pltpu.SemaphoreType.DMA((2, 2, cols // LANES)),
             pltpu.SemaphoreType.DMA((2, 2, cols // LANES)),
+            pltpu.SemaphoreType.DMA((2, max(1, cols // LANES // DETOUR[0]))),
+            pltpu.SemaphoreType.DMA((2, max(1, cols // LANES // DETOUR[0]))),
+            pltpu.SemaphoreType.DMA((max(1, cols // LANES // DETOUR[0]),)),
             pltpu.SemaphoreType.DMA((states,)),
             pltpu.SemaphoreType.DMA((states,)),
         ],

time: 98 us -> 91.2 us (0.931)
  the two profiles are of different devices: /device:TPU:119 before, /device:TPU:39 now
where the time goes in v3:
time: 91.2 us; the launch traced here: 91 us
  Pallas kernels  89.4 us (98%)
  local copies, waits for them, and re-layouts  1.67 us (2%)
    pallas_call x1, Pallas kernels, per_device(): pl.pallas_call(kernel, out_shape=pltpu.VMEM(potential.shape, F32), in_spe...  89.4 us

profile of v3, /device:TPU:39, one launch (start us, length us, event | category | flops | bytes accessed | tf_op | source)
XLA Modules:
  0.0 91.0 jit_solution(17771552213280442311)
XLA Ops:
  0.0 89.4 %lensing.1 = f32[12,32,2048]{2,1,0:T(8,128)S(1)} custom-call(s32[12]{0:T(128)} %width_ref.1, s32[12]{0:T(128)} %slot_ref.1, f32[16]{0:T(128)} %near_ref.1, f32[16]{0:T(128)} %lens_ref.1, f32[12,32,2048]{2,1,0:T(8,128)} %pot_ref.1), custom_call_target="tpu_custom_call" | custom-call | tf_op jit(solution)/shard_map/lensing/pallas_call | solution.py:369
  89.4 1.7 %copy.7 = f32[12,32,2048]{2,1,0:T(8,128)} copy(f32[12,32,2048]{2,1,0:T(8,128)S(1)} %lensing.1) | data formatting | bytes 6291456

commit v4 on v3

--- a/solution.py
+++ b/solution.py
@@ -12,7 +12,7 @@
 SPAN = 128
 FAR = 1000
 PAIR = 2
-DETOUR = (2, 4)
+DETOUR = (6, 3)
 MESH = pl.DeviceIdType.MESH
 F32 = jnp.float32
 BF16 = jnp.bfloat16
@@ -32,9 +32,9 @@
 
 
 def kernel(
-    width_ref, slot_ref, near_ref, lens_ref, pot_ref, out_ref,
-    own, top, bot, pack, relay, nears, strengths, rowm, colm, along, coef, arrived, leaving,
-    load_sem, halo_send, halo_recv, relay_send, relay_recv, forward_send, state_send, state_recv,
+    width_hbm, slot_hbm, near_hbm, lens_hbm, pot_ref, out_ref,
+    width_ref, slot_ref, near_ref, lens_ref, own, top, bot, pack, relay, nears, strengths, rowm, colm, along, coef, arrived, leaving,
+    load_sem, table_sem, halo_send, halo_recv, relay_send, relay_recv, forward_send, state_send, state_recv,
 ):
     depth, sky = lax.axis_index("depth"), lax.axis_index("sky")
     has_before, has_after = sky > 0, sky < lax.axis_size("sky") - 1
@@ -46,13 +46,20 @@
     units = parts * bands
     middle = pl.ds(LANES, cols)
 
-    load = pltpu.make_async_copy(pot_ref, own.at[:, :, middle], load_sem)
-    load.start()
+    edges = ((WMAX, rows - 2 * WMAX), (0, WMAX), (rows - WMAX, WMAX))
+    loads = [
+        pltpu.make_async_copy(pot_ref.at[:, pl.ds(*part), :], own.at[:, pl.ds(*part), middle], load_sem.at[i])
+        for i, part in enumerate(edges)]
+    tables = [
+        pltpu.make_async_copy(*pair, table_sem.at[i]) for i, pair in enumerate((
+            (width_hbm, width_ref), (slot_hbm, slot_ref), (near_hbm, near_ref), (lens_hbm, lens_ref)))]
+    for copy in loads + tables:
+        copy.start()
     x, x_size = depth // PAIR, lax.axis_size("depth") // PAIR
     mirror = depth + PAIR * (x_size - 1 - 2 * x)
     detours, relays = x < x_size // 2, x >= x_size - x_size // 2
     at_end = (x == 0) | (x == x_size - 1)
-    detoured = jnp.where(at_end, pieces // DETOUR[0], pieces // DETOUR[1])
+    detoured = jnp.where(at_end, pieces * DETOUR[0] // 16, pieces * DETOUR[1] // 16)
     first = pieces - detoured
     odd = sky % 2 == 1
     leaves = (odd & has_after, jnp.logical_not(odd) & has_before)
@@ -80,7 +87,7 @@
         def _(buffer=buffer):
             buffer[...] = jnp.zeros_like(buffer)
     pack[...] = jnp.zeros_like(pack)
-    load.wait()
+    loads[0].wait()
     for side, row in ((0, rows - WMAX - 1), (1, WMAX)):
         for k in range(planes):
             pack[side, k // EIGHT, pl.ds(k % EIGHT, 1), :] = own[k, pl.ds(row, 1), middle]
@@ -138,18 +145,22 @@
                     return carry
                 lax.fori_loop(0, detoured, one, 0)
 
-    def each_direct(act):
+    def direct(piece, act):
+        for side in (0, 1):
+            @pl.when(sends[side] & jnp.logical_not(detours & leaves[side] & (piece >= first)))
+            def _(side=side):
+                act(halo(side, 0, piece))
+                act(halo(side, 1, piece))
+
+    def each_direct(act, count):
         def one(piece, carry):
-            for side in (0, 1):
-                @pl.when(sends[side] & jnp.logical_not(detours & leaves[side] & (piece >= first)))
-                def _(side=side):
-                    act(halo(side, 0, piece))
-                    act(halo(side, 1, piece))
+            direct(piece, act)
             return carry
-        lax.fori_loop(0, pieces, one, 0)
+        lax.fori_loop(0, count, one, 0)
 
     each_detoured(lambda copy: copy.start())
-    each_direct(lambda copy: copy.start())
+    early = jnp.where(relays & at_end, pieces // 2, pieces)
+    each_direct(lambda copy: copy.start(), early)
 
     def pass_on(index):
         for side in (0, 1):
@@ -208,7 +219,11 @@
         colm[k] = inside(gap - LANES // 2, half_width).astype(BF16)
         return carry
 
+    for copy in tables:
+        copy.wait()
     lax.fori_loop(0, planes, build, 0)
+    for copy in loads[1:]:
+        copy.wait()
 
     def along_rows(chunk, k):
         window = pl.ds(pl.multiple_of(chunk * TILE, TILE), TILE)
@@ -335,14 +350,19 @@
 
         @pl.when(builds)
         def _():
-            pass_on(turn)
+            pass_on(2 * turn)
+            pass_on(2 * turn + 1)
+            for later in (early + 2 * turn, early + 2 * turn + 1):
+                @pl.when(later < pieces)
+                def _(later=later):
+                    direct(later, lambda copy: copy.start())
 
         return carry
 
     lax.fori_loop(0, tiles + lead, step, 0)
 
     each_detoured(lambda copy: copy.wait_send())
-    each_direct(lambda copy: copy.wait_send())
+    each_direct(lambda copy: copy.wait_send(), pieces)
 
     @pl.when(relays & outside)
     def _():
@@ -365,18 +385,22 @@
     wide = cols + 2 * LANES
     tall = rows + 2 * WMAX + 2 * EIGHT * ninth
     states = (cols // SPAN) * (rows // EIGHT)
-    smem = pl.BlockSpec(memory_space=pltpu.SMEM)
+    table = ratio_near.shape[0]
     return pl.pallas_call(
         kernel,
         out_shape=pltpu.VMEM(potential.shape, F32),
-        in_specs=[smem, smem, smem, smem, pl.BlockSpec(memory_space=pl.ANY)],
+        in_specs=[pl.BlockSpec(memory_space=pl.ANY)] * 5,
         out_specs=pl.BlockSpec(memory_space=pltpu.VMEM),
         scratch_shapes=[
+            pltpu.SMEM((planes,), jnp.int32),
+            pltpu.SMEM((planes,), jnp.int32),
+            pltpu.SMEM((table,), F32),
+            pltpu.SMEM((table,), F32),
             pltpu.VMEM((planes, rows, wide), F32),
             pltpu.VMEM((planes + ninth, EIGHT, wide), F32),
             pltpu.VMEM((planes + ninth, EIGHT, wide), F32),
             pltpu.VMEM((2, ninth, EIGHT, cols), F32),
-            pltpu.VMEM((max(1, cols // LANES // DETOUR[0]), planes + ninth, EIGHT, LANES), F32),
+            pltpu.VMEM((max(1, cols // LANES * DETOUR[0] // 16), planes + ninth, EIGHT, LANES), F32),
             pltpu.SMEM((planes,), F32),
             pltpu.SMEM((planes,), F32),
             pltpu.VMEM((planes, 3 * rows, 2 * tall), BF16),
@@ -385,12 +409,13 @@
             pltpu.VMEM((planes, 3, rows, cols), F32),
             pltpu.VMEM((states, 8, EIGHT, SPAN), F32),
             pltpu.VMEM((states, 8, EIGHT, SPAN), F32),
-            pltpu.SemaphoreType.DMA,
+            pltpu.SemaphoreType.DMA((3,)),
+            pltpu.SemaphoreType.DMA((4,)),
             pltpu.SemaphoreType.DMA((2, 2, cols // LANES)),
             pltpu.SemaphoreType.DMA((2, 2, cols // LANES)),
-            pltpu.SemaphoreType.DMA((2, max(1, cols // LANES // DETOUR[0]))),
-            pltpu.SemaphoreType.DMA((2, max(1, cols // LANES // DETOUR[0]))),
-            pltpu.SemaphoreType.DMA((max(1, cols // LANES // DETOUR[0]),)),
+            pltpu.SemaphoreType.DMA((2, max(1, cols // LANES * DETOUR[0] // 16))),
+            pltpu.SemaphoreType.DMA((2, max(1, cols // LANES * DETOUR[0] // 16))),
+            pltpu.SemaphoreType.DMA((max(1, cols // LANES * DETOUR[0] // 16),)),
             pltpu.SemaphoreType.DMA((states,)),
             pltpu.SemaphoreType.DMA((states,)),
         ],

time: 91.2 us -> 88.6 us (0.971)
  the two profiles are of different devices: /device:TPU:39 before, /device:TPU:119 now
where the time goes in v4:
time: 88.6 us; the launch traced here: 88.5 us
  Pallas kernels  86.8 us (98%)
  local copies, waits for them, and re-layouts  1.67 us (2%)
    pallas_call x1, Pallas kernels, per_device(): pl.pallas_call(kernel, out_shape=pltpu.VMEM(potential.shape, F32), in_spe...  86.8 us

profile of v4, /device:TPU:119, one launch (start us, length us, event | category | flops | bytes accessed | tf_op | source)
XLA Modules:
  0.0 88.5 jit_solution(4561039782206347311)
XLA Ops:
  0.0 86.8 %lensing.1 = f32[12,32,2048]{2,1,0:T(8,128)S(1)} custom-call(s32[12]{0:T(128)} %width_hbm.1, s32[12]{0:T(128)} %slot_hbm.1, f32[16]{0:T(128)} %near_hbm.1, f32[16]{0:T(128)} %lens_hbm.1, f32[12,32,2048]{2,1,0:T(8,128)} %pot_ref.1), custom_call_target="tpu_custom_call" | custom-call | tf_op jit(solution)/shard_map/lensing/pallas_call | solution.py:389
  86.9 1.7 %copy.7 = f32[12,32,2048]{2,1,0:T(8,128)} copy(f32[12,32,2048]{2,1,0:T(8,128)S(1)} %lensing.1) | data formatting | bytes 6291456

commit v5 on v4

--- a/solution.py
+++ b/solution.py
@@ -318,7 +318,18 @@
         return carry
 
     lax.fori_loop(0, planes, rows_first, 0, unroll=4)
-    lead = jnp.clip(depth, 1, tiles)
+    def finish_halos():
+        each_detoured(lambda copy: copy.wait_send())
+        each_direct(lambda copy: copy.wait_send(), pieces)
+
+        @pl.when(relays & outside)
+        def _():
+            def finish(index, carry):
+                forward(0, index).wait_send()
+                return carry
+            lax.fori_loop(0, detoured, finish, 0)
+
+    lead = jnp.clip(depth - (depth > 3).astype(jnp.int32), 1, tiles)
 
     def step(turn, carry):
         builds, moves = turn < tiles, turn >= lead
@@ -330,6 +341,10 @@
             @pl.when(turn < tiles - 1)
             def _():
                 await_halo(2 * turn + 2)
+
+        @pl.when(turn == tiles + lead - 1)
+        def _():
+            finish_halos()
 
         def share(band, carry):
             @pl.when(moves)
@@ -360,16 +375,6 @@
         return carry
 
     lax.fori_loop(0, tiles + lead, step, 0)
-
-    each_detoured(lambda copy: copy.wait_send())
-    each_direct(lambda copy: copy.wait_send(), pieces)
-
-    @pl.when(relays & outside)
-    def _():
-        def finish(index, carry):
-            forward(0, index).wait_send()
-            return carry
-        lax.fori_loop(0, detoured, finish, 0)
 
     @pl.when(gives)
     def _():

time: 88.6 us -> 87.9 us (level)
  Pallas kernels: 86.8 us -> 85.7 us
    pallas_call x1, Pallas kernels: 86.8 us -> 85.7 us  [per_device(): pl.pallas_call(kernel, out_shape=pltpu.VMEM(potential.shape, F32), in_spe...]
where the time goes in v5:
time: 87.9 us; the launch traced here: 87.4 us
  Pallas kernels  85.7 us (97%)
  local copies, waits for them, and re-layouts  1.67 us (2%)
    pallas_call x1, Pallas kernels, per_device(): pl.pallas_call(kernel, out_shape=pltpu.VMEM(potential.shape, F32), in_spe...  85.7 us

profile of v5, /device:TPU:119, one launch (start us, length us, event | category | flops | bytes accessed | tf_op | source)
XLA Modules:
  0.0 87.4 jit_solution(7317020101347636784)
XLA Ops:
  0.0 85.7 %lensing.1 = f32[12,32,2048]{2,1,0:T(8,128)S(1)} custom-call(s32[12]{0:T(128)} %width_hbm.1, s32[12]{0:T(128)} %slot_hbm.1, f32[16]{0:T(128)} %near_hbm.1, f32[16]{0:T(128)} %lens_hbm.1, f32[12,32,2048]{2,1,0:T(8,128)} %pot_ref.1), custom_call_target="tpu_custom_call" | custom-call | tf_op jit(solution)/shard_map/lensing/pallas_call | solution.py:394
  85.7 1.7 %copy.7 = f32[12,32,2048]{2,1,0:T(8,128)} copy(f32[12,32,2048]{2,1,0:T(8,128)S(1)} %lensing.1) | data formatting | bytes 6291456

commit v6 on v5

--- a/solution.py
+++ b/solution.py
@@ -329,7 +329,7 @@
                 return carry
             lax.fori_loop(0, detoured, finish, 0)
 
-    lead = jnp.clip(depth - (depth > 3).astype(jnp.int32), 1, tiles)
+    lead = jnp.clip(depth - (depth > 3).astype(jnp.int32) - (depth > 5).astype(jnp.int32), 1, tiles)
 
     def step(turn, carry):
         builds, moves = turn < tiles, turn >= lead

time: 87.9 us -> 87.9 us (level)
  no operation moved by 1% of the time
where the time goes in v6:
time: 87.9 us; the launch traced here: 87.4 us
  Pallas kernels  85.7 us (97%)
  local copies, waits for them, and re-layouts  1.67 us (2%)
    pallas_call x1, Pallas kernels, per_device(): pl.pallas_call(kernel, out_shape=pltpu.VMEM(potential.shape, F32), in_spe...  85.7 us

profile of v6, /device:TPU:119, one launch (start us, length us, event | category | flops | bytes accessed | tf_op | source)
XLA Modules:
  0.0 87.4 jit_solution(9112144319767331017)
XLA Ops:
  0.0 85.7 %lensing.1 = f32[12,32,2048]{2,1,0:T(8,128)S(1)} custom-call(s32[12]{0:T(128)} %width_hbm.1, s32[12]{0:T(128)} %slot_hbm.1, f32[16]{0:T(128)} %near_hbm.1, f32[16]{0:T(128)} %lens_hbm.1, f32[12,32,2048]{2,1,0:T(8,128)} %pot_ref.1), custom_call_target="tpu_custom_call" | custom-call | tf_op jit(solution)/shard_map/lensing/pallas_call | solution.py:394
  85.7 1.7 %copy.7 = f32[12,32,2048]{2,1,0:T(8,128)} copy(f32[12,32,2048]{2,1,0:T(8,128)S(1)} %lensing.1) | data formatting | bytes 6291456
